TPU v7x, 32 devices: a whole 2x2x4 slice. The times are simulated.
32 devices in a mesh: layer: 2 (over x), expert: 4 (over y, core), col: 4 (over z).
Axes of the slice: x: 2, y: 2, z: 4, core: 2. Of those that a mesh axis runs over, the one named last changes fastest.
Arguments:
- target_weights: bfloat16 [8, 7168, 2048], P(('layer', 'expert'), None, 'col'), parts along dimension 0, may hold values from -36 to 36
- factors: float32 [8, 7168, 128], P(('layer', 'expert'), 'col'), parts along dimension 0, may hold values from -0.5 to 0.5
- bases: float32 [64, 128, 2048], P('layer', None, 'col'), parts along dimension 0, may hold values from -6 to 6
- coefficients: float32 [8, 32], P(('layer', 'expert')), parts along dimension 0, may hold values from -1 to 1
Outputs:
- new_factors: float32 [8, 7168, 128], P(('layer', 'expert'), 'col'), parts along dimension 0
- new_bases: float32 [64, 128, 2048], P('layer', None, 'col'), parts along dimension 0
- new_coefficients: float32 [8, 32], P(('layer', 'expert')), parts along dimension 0
- losses: float32 [4], P('layer'), parts along dimension 0
There are 2 independent parts, one for each index of `layer`. A program takes and returns all parts, laid end to end along the dimension named above; each array names one. Nothing has to cross between parts.
All inputs are finite; a program needn't handle non-finite values.
Results may differ from a plain program's by a relative error of at most 0.0003.
Values sent between devices are 32-bit elements; how exact they have to be, the bound alone decides.
A program may use at most 128 MiB of HBM per device.

v0:
```python
import jax
import jax.numpy as jnp
from jax import lax
from jax.sharding import PartitionSpec as P

D = 7168
H = 2048
ITERS = 2
LEARN_RATE = 0.01
BETA_ONE = 0.9
BETA_TWO = 0.999
EPSILON = 0.0001
HIGHEST = lax.Precision.HIGHEST


def adam_update(parameter, gradient, moment_one, moment_two, iteration):
    moment_one = BETA_ONE * moment_one + (1.0 - BETA_ONE) * gradient
    moment_two = BETA_TWO * moment_two + (1.0 - BETA_TWO) * gradient * gradient
    first_hat = moment_one / (1.0 - BETA_ONE ** (iteration + 1))
    second_hat = moment_two / (1.0 - BETA_TWO ** (iteration + 1))
    parameter = parameter - LEARN_RATE * first_hat / (jnp.sqrt(second_hat) + EPSILON)
    return (parameter, moment_one, moment_two)


def shards(target_weights, factors, bases, coefficients):
    expert_count = lax.axis_size("expert")
    local_experts = target_weights.shape[0]
    basis_share = bases.shape[0] // expert_count
    basis_begin = lax.axis_index("expert") * basis_share
    loss_scale = 1.0 / (2.0 * local_experts * expert_count * D * H)
    own_bases = lax.dynamic_slice_in_dim(bases, basis_begin, basis_share, 0)
    basis_one = jnp.zeros_like(own_bases)
    basis_two = jnp.zeros_like(own_bases)
    coef_one = jnp.zeros_like(coefficients)
    coef_two = jnp.zeros_like(coefficients)
    current_bases = bases
    current_factors = factors
    factor_one = jnp.zeros_like(factors)
    factor_two = jnp.zeros_like(factors)
    loss_values = []
    for iteration in range(ITERS):
        gathered = lax.all_gather(current_factors, "col", axis=1, tiled=True)
        mixed = jnp.tanh(jnp.einsum("ek,krh->erh", coefficients, current_bases, precision=HIGHEST))
        residual = jnp.einsum(
            "edr,erh->edh", gathered, mixed, precision=HIGHEST
        ) - target_weights.astype(jnp.float32)
        loss_part = jnp.sum(residual * residual)
        gradient = residual / H
        d_mixed = jnp.einsum("edr,edh->erh", gathered, gradient, precision=HIGHEST)
        d_pre = d_mixed * (1.0 - mixed * mixed)
        coef_slice = coefficients
        d_basis = lax.psum_scatter(
            jnp.einsum("ek,erh->krh", coef_slice, d_pre, precision=HIGHEST),
            "expert",
            scatter_dimension=0,
            tiled=True,
        )
        d_coef = lax.psum(jnp.einsum("krh,erh->ek", current_bases, d_pre, precision=HIGHEST), "col")
        d_share = lax.psum_scatter(
            jnp.einsum("edh,erh->der", gradient, mixed, precision=HIGHEST),
            "col",
            scatter_dimension=0,
            tiled=True,
        )
        d_share = jnp.transpose(d_share, (1, 0, 2))
        current_factors, factor_one, factor_two = adam_update(
            current_factors, d_share, factor_one, factor_two, iteration
        )
        own_bases, basis_one, basis_two = adam_update(
            own_bases, d_basis, basis_one, basis_two, iteration
        )
        coefficients, coef_one, coef_two = adam_update(
            coefficients, d_coef, coef_one, coef_two, iteration
        )
        current_bases = lax.all_gather(own_bases, "expert", axis=0, tiled=True)
        loss_values.append(lax.psum(loss_part, ("expert", "col")))
    loss_totals = jnp.stack(loss_values)
    return (current_factors, current_bases, coefficients, loss_totals * loss_scale)


def solution(mesh):
    return jax.shard_map(
        shards,
        mesh=mesh,
        in_specs=(
            P(("layer", "expert"), None, "col"),
            P(("layer", "expert"), "col", None),
            P("layer", None, "col"),
            P(("layer", "expert"), None),
        ),
        out_specs=(
            P(("layer", "expert"), "col", None),
            P("layer", None, "col"),
            P(("layer", "expert"), None),
            P("layer"),
        ),
        check_vma=False,
    )
```

profile of v0, /device:TPU:0, one launch (start us, length us, event | category | flops | bytes accessed | tf_op | source)
XLA Modules:
  0.0 658.7 jit_solution(1172919864465616903)
XLA Ops:
  7.9 12.3 %fusion.20 = f32[1,128,512]{2,0,1:T(1,128)S(1)} fusion(f32[32,128,512]{2,1,0:T(8,128)} %param.6, f32[1,32]{1,0:T(1,128)} %param.7), kind=kOutput, calls=%fused_computation.20 | convolution fusion | flops 25165824 | bytes 8650880 | tf_op jit(solution)/shard_map/ek,krh->erh/dot_general | solution.py:43
  20.4 10.1 %copy.15 = bf16[1,7168,512]{1,2,0:T(8,128)(2,1)} copy(bf16[1,7168,512]{2,1,0:T(8,128)(2,1)} %param.4) | data formatting | bytes 14680064 | tf_op args[0]
  30.4 54.0 %all-gather.5.cloned.1.call-done = f32[1,7168,128]{2,1,0:T(8,128)} async-done(((f32[1,1792,128]{2,1,0:T(8,128)}), f32[1,7168,128]{2,1,0:T(8,128)}) %all-gather.5.cloned.1.call-update) | async-done | bytes 3670032 | tf_op jit(solution)/shard_map/all_gather | solution.py:42
  84.4 19.3 %multiply_reduce_fusion.1 = (f32[]{:T(128)}, f32[1,7168,512]{1,2,0:T(8,128)S(1)}) fusion(bf16[1,7168,512]{1,2,0:T(8,128)(2,1)} %copy.15, f32[1,7168,128]{2,1,0:T(8,128)} %all-gather.5.cloned.1.call-done, f32[1,128,512]{1,2,0:T(8,128)S(1)} %copy.23), kind=kOutput, calls=%fused_computation.11 | convolution fusion | flops 5651824640 | bytes 25952260 | tf_op jit(solution)/shard_map/edr,erh->edh/dot_general | solution.py:44
  103.7 5.2 copy-done.1
  108.9 11.7 %fusion.41 = f32[128,512]{0,1:T(8,128)S(1)} fusion(f32[1,7168,128]{2,1,0:T(8,128)S(1)} %copy-done.4, f32[1,7168,512]{1,2,0:T(8,128)S(1)} %get-tuple-element.17, f32[1,128,512]{1,2,0:T(8,128)S(1)} %copy.23), kind=kOutput, calls=%fused_computation.44 | convolution fusion | flops 5641011200 | bytes 18874368 | tf_op jit(solution)/shard_map/edr,edh->erh/dot_general | solution.py:49
  120.8 4.5 multiply_bitcast_fusion
  125.4 13.9 %fusion.12 = f32[7168,1,128]{0,2,1:T(8,128)} fusion(f32[1,7168,512]{1,2,0:T(8,128)} %copy-done.1, f32[1,128,512]{1,2,0:T(8,128)S(1)} %copy.23), kind=kOutput, calls=%fused_computation.16 | convolution fusion | flops 5640814592 | bytes 18612224 | tf_op jit(solution)/shard_map/edh,erh->der/dot_general | solution.py:60
  139.3 56.1 %reduce-scatter.7.cloned.1.call-done = f32[8,128,512]{2,1,0:T(8,128)} async-done(((f32[32,128,512]{2,1,0:T(8,128)}), f32[8,128,512]{2,1,0:T(8,128)}) %reduce-scatter.7.cloned.1.call-update) | async-done | bytes 2097168 | tf_op jit(solution)/shard_map/reduce_scatter | solution.py:52
  195.4 4.6 divide_subtract_fusion
  200.4 65.9 %reduce-scatter.5.cloned.1.call-done = f32[1792,1,128]{0,2,1:T(8,128)} async-done(((f32[7168,1,128]{0,2,1:T(8,128)}), f32[1792,1,128]{0,2,1:T(8,128)}) %reduce-scatter.5.cloned.1.call-update) | async-done | bytes 917520 | tf_op jit(solution)/shard_map/reduce_scatter | solution.py:59
  266.3 2.6 fusion.60
  268.9 10.5 %copy.25 = f32[32,128,512]{1,0,2:T(8,128)} copy(f32[32,128,512]{2,1,0:T(8,128)} %param.6) | data formatting | bytes 16777216 | tf_op args[2]
  279.5 9.3 %convolution_bitcast_fusion.1 = f32[1,32]{1,0:T(1,128)S(1)} fusion(f32[128,512,1]{0,2,1:T(1,128)S(1)} %bitcast.131, f32[32,128,512]{1,0,2:T(8,128)} %copy.25), kind=kOutput, calls=%fused_computation.47 | convolution fusion | flops 25165824 | bytes 8650880 | tf_op jit(solution)/shard_map/krh,erh->ek/dot_general | solution.py:58
  288.8 11.5 %psum.28 = f32[1,32]{1,0:T(1,128)S(1)} all-reduce(f32[1,32]{1,0:T(1,128)S(1)} %convolution_bitcast_fusion.1), channel_id=1, replica_groups=mesh['layer'=2,'expert'=4,'col'=4] {'col'}, use_global_device_ids=true, to_apply=%region_1.0 | all-reduce | flops 32 | bytes 256 | tf_op jit(solution)/shard_map/psum | solution.py:58
  300.3 26.0 %all-gather.7.cloned.1.call-done = f32[32,128,512]{2,1,0:T(8,128)} async-done(((f32[8,128,512]{2,1,0:T(8,128)}), f32[32,128,512]{2,1,0:T(8,128)}) %all-gather.7.cloned.1.call-update) | async-done | bytes 8388624 | tf_op jit(solution)/shard_map/all_gather | solution.py:75
  326.3 12.3 %fusion.18 = f32[1,128,512]{2,0,1:T(1,128)S(1)} fusion(f32[32,128,512]{2,1,0:T(8,128)} %all-gather.7.cloned.1.call-done, f32[1,32]{1,0:T(1,128)S(1)} %divide_subtract_fusion.2), kind=kOutput, calls=%fused_computation.18 | convolution fusion | flops 25165824 | bytes 8650880 | tf_op jit(solution)/shard_map/ek,krh->erh/dot_general | solution.py:43
  338.7 61.7 %all-gather.9.cloned.1.call-done = f32[1,7168,128]{1,2,0:T(8,128)} async-done(((f32[1,1792,128]{1,2,0:T(8,128)}), f32[1,7168,128]{1,2,0:T(8,128)}) %all-gather.9.cloned.1.call-update) | async-done | bytes 3670032 | tf_op jit(solution)/shard_map/all_gather | solution.py:42
  400.4 18.9 %multiply_reduce_fusion = (f32[]{:T(128)}, f32[1,7168,512]{1,2,0:T(8,128)S(1)}) fusion(bf16[1,7168,512]{1,2,0:T(8,128)(2,1)} %copy.15, f32[1,128,512]{1,2,0:T(8,128)S(1)} %copy.27, f32[1,7168,128]{1,2,0:T(8,128)} %all-gather.9.cloned.1.call-done), kind=kOutput, calls=%fused_computation.10 | convolution fusion | flops 5651824640 | bytes 25952260 | tf_op jit(solution)/shard_map/edr,erh->edh/dot_general | solution.py:44
  419.3 5.2 copy-done
  424.5 11.7 %fusion.46 = f32[128,512]{0,1:T(8,128)S(1)} fusion(f32[1,7168,512]{1,2,0:T(8,128)S(1)} %get-tuple-element.15, f32[1,7168,128]{1,2,0:T(8,128)S(1)} %copy-done.2, f32[1,128,512]{1,2,0:T(8,128)S(1)} %copy.27), kind=kOutput, calls=%fused_computation.45 | convolution fusion | flops 5641011200 | bytes 18874368 | tf_op jit(solution)/shard_map/edr,edh->erh/dot_general | solution.py:49
  436.3 4.5 broadcast_multiply_fusion
  440.9 14.0 %fusion.15 = f32[7168,1,128]{0,2,1:T(8,128)} fusion(f32[1,7168,512]{1,2,0:T(8,128)} %copy-done, f32[1,128,512]{1,2,0:T(8,128)S(1)} %copy.27), kind=kOutput, calls=%fused_computation.17 | convolution fusion | flops 5640814592 | bytes 18612224 | tf_op jit(solution)/shard_map/edh,erh->der/dot_general | solution.py:60
  455.0 56.0 %reduce-scatter.11.cloned.1.call-done = f32[8,128,512]{2,1,0:T(8,128)} async-done(((f32[32,128,512]{2,1,0:T(8,128)}), f32[8,128,512]{2,1,0:T(8,128)}) %reduce-scatter.11.cloned.1.call-update) | async-done | bytes 2097168 | tf_op jit(solution)/shard_map/reduce_scatter | solution.py:52
  511.0 5.1 fusion.35
  516.1 35.0 %all-reduce = (f32[1]{0:T(128)}, f32[1]{0:T(128)}) all-reduce(f32[1]{0:T(128)} %bitcast.30, f32[1]{0:T(128)} %bitcast.29), channel_id=1, replica_groups=mesh['layer'=2,'expert'=4,'col'=4] {'expert','col'}, use_global_device_ids=true, to_apply=%region_9.0 | all-reduce | flops 2 | bytes 16 | tf_op jit(solution)/shard_map/psum | solution.py:76
  551.1 10.2 %copy.31 = f32[32,128,512]{1,0,2:T(8,128)} copy(f32[32,128,512]{2,1,0:T(8,128)} %all-gather.7.cloned.1.call-done) | data formatting | bytes 16777216 | tf_op jit(solution)/shard_map/all_gather | solution.py:75
  561.3 9.0 %convolution_bitcast_fusion = f32[1,32]{1,0:T(1,128)S(1)} fusion(f32[128,512,1]{0,2,1:T(1,128)S(1)} %bitcast.132, f32[32,128,512]{1,0,2:T(8,128)} %copy.31), kind=kOutput, calls=%fused_computation.46 | convolution fusion | flops 25165824 | bytes 8650880 | tf_op jit(solution)/shard_map/krh,erh->ek/dot_general | solution.py:58
  570.3 9.2 %psum.29 = f32[1,32]{1,0:T(1,128)S(1)} all-reduce(f32[1,32]{1,0:T(1,128)S(1)} %convolution_bitcast_fusion), channel_id=1, replica_groups=mesh['layer'=2,'expert'=4,'col'=4] {'col'}, use_global_device_ids=true, to_apply=%region_5.0 | all-reduce | flops 32 | bytes 256 | tf_op jit(solution)/shard_map/psum | solution.py:58
  583.2 2.2 fusion.56
  586.6 56.6 %all-gather.11.cloned.1.call-done = f32[32,128,512]{2,1,0:T(8,128)} async-done(((f32[8,128,512]{2,1,0:T(8,128)}), f32[32,128,512]{2,1,0:T(8,128)}) %all-gather.11.cloned.1.call-update) | async-done | bytes 8388624 | tf_op jit(solution)/shard_map/all_gather | solution.py:75
  643.3 8.4 %copy.37 = f32[32,128,512]{2,1,0:T(8,128)} copy(f32[32,128,512]{2,1,0:T(8,128)} %all-gather.11.cloned.1.call-done) | data formatting | bytes 16777216
  (40 shorter events, 6.8 us)
Async XLA Ops:
  7.2 77.2 %all-gather.5.cloned.1.call-start = ((), (), s32[]{:S(2)}) async-start(), calls=%async_computation.4 | async-start | bytes 4587520 | tf_op jit(solution)/shard_map/all_gather | solution.py:42
  7.9 187.5 %reduce-scatter.7.cloned.1.call-start = ((), (), s32[]{:S(2)}) async-start(), calls=%async_computation.6 | async-start | bytes 10485760 | tf_op jit(solution)/shard_map/reduce_scatter | solution.py:52
  84.4 24.5 %copy-start.4 = (f32[1,7168,128]{2,1,0:T(8,128)S(1)}, f32[1,7168,128]{2,1,0:T(8,128)}, u32[]{:S(2)}) copy-start(f32[1,7168,128]{2,1,0:T(8,128)} %all-gather.5.cloned.1.call-done) | copy-start | bytes 11010052
  103.7 5.2 copy-start.1
  108.9 11.9 %copy-start.7 = (f32[1,32]{1,0:T(1,128)S(1)}, f32[1,32]{1,0:T(1,128)}, u32[]{:S(2)}) copy-start(f32[1,32]{1,0:T(1,128)} %param.7) | copy-start | bytes 388
  125.3 141.0 %reduce-scatter.5.cloned.1.call-start = ((), (), s32[]{:S(2)}) async-start(), calls=%async_computation.5 | async-start | bytes 4587520 | tf_op jit(solution)/shard_map/reduce_scatter | solution.py:59
  139.2 60.9 %copy-start.5 = (f32[1,1792,128]{2,1,0:T(8,128)S(1)}, f32[1,1792,128]{2,1,0:T(8,128)}, u32[]{:S(2)}) copy-start(f32[1,1792,128]{2,1,0:T(8,128)} %param.5) | copy-start | bytes 2752516
  139.2 187.0 %all-gather.7.cloned.1.call-start = ((), (), s32[]{:S(2)}) async-start(), calls=%async_computation.7 | async-start | bytes 10485760 | tf_op jit(solution)/shard_map/all_gather | solution.py:75
  200.0 200.4 %all-gather.9.cloned.1.call-start = ((), (), s32[]{:S(2)}) async-start(), calls=%async_computation.8 | async-start | bytes 4587520 | tf_op jit(solution)/shard_map/all_gather | solution.py:42
  268.9 242.1 %reduce-scatter.11.cloned.1.call-start = ((), (), s32[]{:S(2)}) async-start(), calls=%async_computation.10 | async-start | bytes 10485760 | tf_op jit(solution)/shard_map/reduce_scatter | solution.py:52
  400.4 24.1 %copy-start.2 = (f32[1,7168,128]{1,2,0:T(8,128)S(1)}, f32[1,7168,128]{1,2,0:T(8,128)}, u32[]{:S(2)}) copy-start(f32[1,7168,128]{1,2,0:T(8,128)} %all-gather.9.cloned.1.call-done) | copy-start | bytes 11010052
  419.3 5.2 copy-start
  440.9 70.1 %copy-start.3 = (f32[8,128,512]{2,1,0:T(8,128)S(1)}, f32[8,128,512]{2,1,0:T(8,128)}, u32[]{:S(2)}) copy-start(f32[8,128,512]{2,1,0:T(8,128)} %divide_subtract_fusion) | copy-start | bytes 6291460
  440.9 142.3 %reduce-scatter.9.cloned.1.call-start = ((), (), s32[]{:S(2)}) async-start(), calls=%async_computation.9 | async-start | bytes 4587520 | tf_op jit(solution)/shard_map/reduce_scatter | solution.py:59
  455.0 188.3 %all-gather.11.cloned.1.call-start = ((), (), s32[]{:S(2)}) async-start(), calls=%async_computation.11 | async-start | bytes 10485760 | tf_op jit(solution)/shard_map/all_gather | solution.py:75
  561.3 21.8 %copy-start.6 = (f32[1792,1,128]{0,2,1:T(8,128)S(1)}, f32[1792,1,128]{0,2,1:T(8,128)}, u32[]{:S(2)}) copy-start(f32[1792,1,128]{0,2,1:T(8,128)} %reduce-scatter.5.cloned.1.call-done) | copy-start | bytes 2752516
Sparse Core Ops, SparseCore 0:
  9.5 74.8 all-gather.4
  125.4 69.9 reduce-scatter.6
  197.7 68.5 reduce-scatter.4
  267.7 58.5 all-gather.6
  328.3 72.0 all-gather.8
  441.0 69.9 reduce-scatter.10
  513.3 69.8 reduce-scatter.8
  584.7 58.5 all-gather.10
where the time goes:
time: 664 us; the launch traced here: 659 us
  waiting for transfers between devices  378 us (57%)
  matrix products  132 us (20%)
  blocking collectives  55.7 us (8%)
  local copies, waits for them, and re-layouts  51.6 us (8%)
  other arithmetic  25.9 us (4%)
  between operations  14.5 us (2%)
    all_gather x2, waiting for transfers between devices, shards(): gathered = lax.all_gather(current_factors, 'col', axis=1, tiled=True)  116 us
    reduce_scatter x2, waiting for transfers between devices, shards(): lax.psum_scatter(jnp.einsum('ek,erh->krh', coef_slice, d_pre, precision=H...  112 us
    all_gather x2, waiting for transfers between devices, shards(): current_bases = lax.all_gather(own_bases, 'expert', axis=0, tiled=True)  82.6 us
    reduce_scatter x2, waiting for transfers between devices, shards(): lax.psum_scatter(jnp.einsum('edh,erh->der', gradient, mixed, precision=HI...  67.1 us
    unnamed x21, local copies, waits for them, and re-layouts  40.9 us
    dot_general x2, matrix products, shards(): jnp.einsum('edr,erh->edh', gathered, mixed, precision=HIGHEST)  38.2 us
    psum x1, blocking collectives, shards(): loss_values.append(lax.psum(loss_part, ('expert', 'col')))  35 us
    dot_general x2, matrix products, shards(): jnp.einsum('edh,erh->der', gradient, mixed, precision=HIGHEST)  27.9 us
  transfers between devices with their start and end apart: 8, of which 8 were waited for; matrix products, arithmetic and copies ran while one was open for 18% of the time, Pallas kernels for 0%

commit v1 on v0

--- a/solution.py
+++ b/solution.py
@@ -11,6 +11,17 @@
 BETA_TWO = 0.999
 EPSILON = 0.0001
 HIGHEST = lax.Precision.HIGHEST
+
+
+def turned_line(block, axis, along):
+    size = lax.axis_size(axis)
+    hops = [(i, (i + 1) % size) for i in range(size)]
+    parts = [block]
+    for reach in range(1, size):
+        parts = [lax.ppermute(parts[0], axis, hops), *parts]
+    out = jnp.concatenate(parts, axis=along)
+    shift = (lax.axis_index(axis) + 1) * parts[-1].shape[along]
+    return jnp.roll(out, shift, axis=along)
 
 
 def adam_update(parameter, gradient, moment_one, moment_two, iteration):
@@ -39,7 +50,7 @@
     factor_two = jnp.zeros_like(factors)
     loss_values = []
     for iteration in range(ITERS):
-        gathered = lax.all_gather(current_factors, "col", axis=1, tiled=True)
+        gathered = turned_line(current_factors, "col", 1)
         mixed = jnp.tanh(jnp.einsum("ek,krh->erh", coefficients, current_bases, precision=HIGHEST))
         residual = jnp.einsum(
             "edr,erh->edh", gathered, mixed, precision=HIGHEST

time: 664 us -> 615 us (0.926)
  local copies, waits for them, and re-layouts: 51.6 us -> 10.8 us
  waiting for transfers between devices: 378 us -> 339 us
  other arithmetic: 25.9 us -> 54.4 us
  matrix products: 132 us -> 118 us
  blocking collectives: 55.7 us -> 64.8 us
    all_gather x2 -> x0, waiting for transfers between devices: 116 us -> none  [shards(): gathered = lax.all_gather(current_factors, 'col', axis=1, tiled=True)]
    ppermute x0 -> x6, waiting for transfers between devices: none -> 101 us  [turned_line(): parts = [lax.ppermute(parts[0], axis, hops), *parts]]
    unnamed x21, local copies, waits for them, and re-layouts: 40.9 us -> 10.8 us
    all_gather x2, waiting for transfers between devices: 82.6 us -> 57.1 us  [shards(): current_bases = lax.all_gather(own_bases, 'expert', axis=0, tiled=True)]
    another operation x0 -> x2, other arithmetic: none -> 20.9 us
    dot_general x2 -> x0, matrix products: 18.3 us -> none  [shards(): jnp.einsum('krh,erh->ek', current_bases, d_pre, precision=HIGHEST)]
    reduce_scatter x2, waiting for transfers between devices: 67.1 us -> 81.2 us  [shards(): lax.psum_scatter(jnp.einsum('edh,erh->der', gradient, mixed, precision=HI...]
    dot_general x2, matrix products: 27.9 us -> 40.1 us  [shards(): jnp.einsum('edh,erh->der', gradient, mixed, precision=HIGHEST)]
  transfers between devices with their start and end apart: 8 -> 12, of which waited for: 8 -> 10; matrix products, arithmetic and copies ran while one was open for 18% -> 14% of each run, Pallas kernels for 0% -> 0%
where the time goes in v1:
time: 615 us; the launch traced here: 607 us
  waiting for transfers between devices  339 us (55%)
  matrix products  118 us (19%)
  blocking collectives  64.8 us (11%)
  other arithmetic  54.4 us (9%)
  between operations  14.4 us (2%)
  local copies, waits for them, and re-layouts  10.8 us (2%)
    ppermute x6, waiting for transfers between devices, turned_line(): parts = [lax.ppermute(parts[0], axis, hops), *parts]  101 us
    reduce_scatter x2, waiting for transfers between devices, shards(): lax.psum_scatter(jnp.einsum('ek,erh->krh', coef_slice, d_pre, precision=H...  99.9 us
    reduce_scatter x2, waiting for transfers between devices, shards(): lax.psum_scatter(jnp.einsum('edh,erh->der', gradient, mixed, precision=HI...  81.2 us
    all_gather x2, waiting for transfers between devices, shards(): current_bases = lax.all_gather(own_bases, 'expert', axis=0, tiled=True)  57.1 us
    dot_general x2, matrix products, shards(): jnp.einsum('edh,erh->der', gradient, mixed, precision=HIGHEST)  40.1 us
    dot_general x2, matrix products, shards(): jnp.einsum('edr,erh->edh', gathered, mixed, precision=HIGHEST)  36 us
    psum x1, blocking collectives, shards(): loss_values.append(lax.psum(loss_part, ('expert', 'col')))  35 us
    psum x2, blocking collectives, shards(): lax.psum(jnp.einsum('krh,erh->ek', current_bases, d_pre, precision=HIGHES...  29.8 us
  transfers between devices with their start and end apart: 12, of which 10 were waited for; matrix products, arithmetic and copies ran while one was open for 14% of the time, Pallas kernels for 0%

profile of v1, /device:TPU:0, one launch (start us, length us, event | category | flops | bytes accessed | tf_op | source)
XLA Modules:
  0.0 607.0 jit_solution(2517056641889840278)
XLA Ops:
  7.2 3.1 collective-permute-start
  10.3 22.6 %collective-permute-done = f32[1,1792,128]{2,1,0:T(8,128)S(1)} collective-permute-done((f32[1,1792,128]{2,1,0:T(8,128)}, f32[1,1792,128]{2,1,0:T(8,128)S(1)}, u32[]{:S(2)}, u32[]{:S(2)}) %collective-permute-start) | collective-permute-done | bytes 917536 | tf_op jit(solution)/shard_map/ppermute | solution.py:21
  32.9 23.3 %collective-permute-done.1 = f32[1,1792,128]{2,1,0:T(8,128)S(1)} collective-permute-done((f32[1,1792,128]{2,1,0:T(8,128)S(1)}, f32[1,1792,128]{2,1,0:T(8,128)S(1)}, u32[]{:S(2)}, u32[]{:S(2)}) %collective-permute-start.1) | collective-permute-done | bytes 917536 | tf_op jit(solution)/shard_map/ppermute | solution.py:21
  56.2 12.4 %fusion.20 = f32[1,128,512]{2,0,1:T(1,128)S(1)} fusion(f32[32,128,512]{2,1,0:T(8,128)} %param.8, f32[1,32]{1,0:T(1,128)} %param.9), kind=kOutput, calls=%fused_computation.22 | convolution fusion | flops 25165824 | bytes 8650880 | tf_op jit(solution)/shard_map/ek,krh->erh/dot_general | solution.py:54
  68.6 10.2 %collective-permute-done.2 = f32[1,1792,128]{2,1,0:T(8,128)} collective-permute-done((f32[1,1792,128]{2,1,0:T(8,128)S(1)}, f32[1,1792,128]{2,1,0:T(8,128)}, u32[]{:S(2)}, u32[]{:S(2)}) %collective-permute-start.2) | collective-permute-done | bytes 917536 | tf_op jit(solution)/shard_map/ppermute | solution.py:21
  78.8 12.0 %fusion.38 = f32[7168,128]{1,0:T(8,128)} fusion(s32[]{:T(128)S(6)} %select_n.17, f32[1,1792,128]{2,1,0:T(8,128)} %collective-permute-done.2, f32[1,1792,128]{2,1,0:T(8,128)S(1)} %collective-permute-done.1, f32[1,1792,128]{2,1,0:T(8,128)S(1)} %collective-permute-done, f32[1,1792,128]{2,1,0:T(8,128)S(1)} %copy-done.6), kind=kLoop, calls=%fused_computation.58 | loop fusion | flops 6422528 | bytes 7340036 | tf_op jit(solution)/shard_map/reshape.2
  90.8 18.3 %multiply_reduce_fusion.1 = (f32[]{:T(128)}, f32[1,7168,512]{2,1,0:T(8,128)S(1)}) fusion(bf16[1,7168,512]{2,1,0:T(8,128)(2,1)} %param.6, f32[7168,128]{1,0:T(8,128)} %fusion.38, f32[1,128,512]{2,0,1:T(1,128)S(1)} %fusion.20), kind=kOutput, calls=%fused_computation.11 | convolution fusion | flops 5651824640 | bytes 25952260 | tf_op jit(solution)/shard_map/edr,erh->edh/dot_general | solution.py:55
  109.1 9.2 %fusion.48 = f32[128,512]{1,0:T(8,128)S(1)} fusion(f32[7168,128]{1,0:T(8,128)S(1)} %copy-done.3, f32[1,7168,512]{2,1,0:T(8,128)S(1)} %get-tuple-element.18, f32[1,128,512]{2,0,1:T(1,128)S(1)} %fusion.20), kind=kOutput, calls=%fused_computation.73 | convolution fusion | flops 5641011200 | bytes 18874368 | tf_op jit(solution)/shard_map/edr,edh->erh/dot_general | solution.py:60
  118.3 4.5 multiply_bitcast_fusion
  122.9 20.1 %fusion.12 = f32[7168,1,128]{0,2,1:T(8,128)} fusion(f32[1,7168,512]{2,1,0:T(8,128)} %copy-done, f32[1,128,512]{2,0,1:T(1,128)S(1)} %fusion.20), kind=kOutput, calls=%fused_computation.16 | convolution fusion | flops 5640814592 | bytes 18612224 | tf_op jit(solution)/shard_map/edh,erh->der/dot_general | solution.py:71
  143.1 49.2 %reduce-scatter.7.cloned.1.call-done = f32[8,128,512]{2,1,0:T(8,128)} async-done(((f32[32,128,512]{2,1,0:T(8,128)}), f32[8,128,512]{2,1,0:T(8,128)}) %reduce-scatter.7.cloned.1.call-update) | async-done | bytes 2097168 | tf_op jit(solution)/shard_map/reduce_scatter | solution.py:63
  192.2 4.6 divide_subtract_fusion
  197.3 65.8 %reduce-scatter.5.cloned.1.call-done = f32[1792,1,128]{0,2,1:T(8,128)} async-done(((f32[7168,1,128]{0,2,1:T(8,128)}), f32[1792,1,128]{0,2,1:T(8,128)}) %reduce-scatter.5.cloned.1.call-update) | async-done | bytes 917520 | tf_op jit(solution)/shard_map/reduce_scatter | solution.py:70
  266.0 22.3 %collective-permute-done.3 = f32[1,1792,128]{1,2,0:T(8,128)S(1)} collective-permute-done((f32[1,1792,128]{1,2,0:T(8,128)S(1)}, f32[1,1792,128]{1,2,0:T(8,128)S(1)}, u32[]{:S(2)}, u32[]{:S(2)}) %collective-permute-start.3) | collective-permute-done | bytes 917536 | tf_op jit(solution)/shard_map/ppermute | solution.py:21
  289.2 22.8 %collective-permute-done.4 = f32[1,1792,128]{1,2,0:T(8,128)} collective-permute-done((f32[1,1792,128]{1,2,0:T(8,128)S(1)}, f32[1,1792,128]{1,2,0:T(8,128)}, u32[]{:S(2)}, u32[]{:S(2)}) %collective-permute-start.4) | collective-permute-done | bytes 917536 | tf_op jit(solution)/shard_map/ppermute | solution.py:21
  312.0 4.2 multiply_reduce_fusion.3
  316.2 19.9 %psum.28 = f32[1,32]{1,0:T(1,128)S(1)} all-reduce(f32[1,32]{1,0:T(1,128)S(1)} %bitcast.106), channel_id=1, replica_groups=mesh['layer'=2,'expert'=4,'col'=4] {'col'}, use_global_device_ids=true, to_apply=%region_1.3 | all-reduce | flops 32 | bytes 256 | tf_op jit(solution)/shard_map/psum | solution.py:69
  336.1 8.9 %fusion.30 = f32[7168,128]{0,1:T(8,128)} fusion(s32[]{:T(128)S(6)} %select_n.17, f32[1,1792,128]{1,2,0:T(8,128)} %collective-permute-done.5, f32[1,1792,128]{1,2,0:T(8,128)} %collective-permute-done.4, f32[1,1792,128]{1,2,0:T(8,128)} %copy-done.7, f32[1,1792,128]{1,2,0:T(8,128)S(1)} %fusion.63), kind=kLoop, calls=%fused_computation.50 | loop fusion | flops 6422528 | bytes 7340036 | tf_op jit(solution)/shard_map/reshape.21
  345.0 12.4 %fusion.18 = f32[1,128,512]{2,0,1:T(1,128)S(1)} fusion(f32[32,128,512]{2,1,0:T(8,128)} %all-gather.3.cloned.1.call-done, f32[1,32]{1,0:T(1,128)S(1)} %divide_subtract_fusion.2), kind=kOutput, calls=%fused_computation.19 | convolution fusion | flops 25165824 | bytes 8650880 | tf_op jit(solution)/shard_map/ek,krh->erh/dot_general | solution.py:54
  357.4 17.7 %multiply_reduce_fusion = (f32[]{:T(128)}, f32[1,7168,512]{2,1,0:T(8,128)S(1)}) fusion(bf16[1,7168,512]{2,1,0:T(8,128)(2,1)} %param.6, f32[7168,128]{0,1:T(8,128)S(1)} %copy-done.2, f32[1,128,512]{2,0,1:T(1,128)S(1)} %fusion.18), kind=kOutput, calls=%fused_computation.10 | convolution fusion | flops 5651824640 | bytes 25952260 | tf_op jit(solution)/shard_map/edr,erh->edh/dot_general | solution.py:55
  375.1 8.4 %fusion.51 = f32[128,512]{1,0:T(8,128)S(1)} fusion(f32[7168,128]{0,1:T(8,128)S(1)} %copy-done.2, f32[1,7168,512]{2,1,0:T(8,128)S(1)} %get-tuple-element.16, f32[1,128,512]{2,0,1:T(1,128)S(1)} %fusion.18), kind=kOutput, calls=%fused_computation.74 | convolution fusion | flops 5641011200 | bytes 18874368 | tf_op jit(solution)/shard_map/edr,edh->erh/dot_general | solution.py:60
  383.5 4.5 broadcast_multiply_fusion
  388.1 20.1 %fusion.15 = f32[7168,1,128]{0,2,1:T(8,128)} fusion(f32[1,7168,512]{2,1,0:T(8,128)} %copy-done.1, f32[1,128,512]{2,0,1:T(1,128)S(1)} %fusion.18), kind=kOutput, calls=%fused_computation.17 | convolution fusion | flops 5640814592 | bytes 18612224 | tf_op jit(solution)/shard_map/edh,erh->der/dot_general | solution.py:71
  408.2 50.7 %reduce-scatter.11.cloned.1.call-done = f32[8,128,512]{2,1,0:T(8,128)} async-done(((f32[32,128,512]{2,1,0:T(8,128)}), f32[8,128,512]{2,1,0:T(8,128)}) %reduce-scatter.11.cloned.1.call-update) | async-done | bytes 2097168 | tf_op jit(solution)/shard_map/reduce_scatter | solution.py:63
  459.0 5.0 fusion.47
  464.0 35.0 %all-reduce = (f32[1]{0:T(128)}, f32[1]{0:T(128)}) all-reduce(f32[1]{0:T(128)} %bitcast.26, f32[1]{0:T(128)} %bitcast.25), channel_id=1, replica_groups=mesh['layer'=2,'expert'=4,'col'=4] {'expert','col'}, use_global_device_ids=true, to_apply=%region_9.11 | all-reduce | flops 2 | bytes 16 | tf_op jit(solution)/shard_map/psum | solution.py:87
  499.0 4.3 multiply_reduce_fusion.2
  503.3 9.9 %psum.29 = f32[1,32]{1,0:T(1,128)S(1)} all-reduce(f32[1,32]{1,0:T(1,128)S(1)} %bitcast.105), channel_id=1, replica_groups=mesh['layer'=2,'expert'=4,'col'=4] {'col'}, use_global_device_ids=true, to_apply=%region_5.7 | all-reduce | flops 32 | bytes 256 | tf_op jit(solution)/shard_map/psum | solution.py:69
  515.6 15.4 %reduce-scatter.9.cloned.1.call-done = f32[1792,1,128]{0,2,1:T(8,128)} async-done(((f32[7168,1,128]{0,2,1:T(8,128)}), f32[1792,1,128]{0,2,1:T(8,128)}) %reduce-scatter.9.cloned.1.call-update) | async-done | bytes 917520 | tf_op jit(solution)/shard_map/reduce_scatter | solution.py:70
  531.0 2.2 fusion.59
  534.5 57.1 %all-gather.5.cloned.1.call-done = f32[32,128,512]{2,1,0:T(8,128)} async-done(((f32[8,128,512]{2,1,0:T(8,128)}), f32[32,128,512]{2,1,0:T(8,128)}) %all-gather.5.cloned.1.call-update) | async-done | bytes 8388624 | tf_op jit(solution)/shard_map/all_gather | solution.py:86
  591.5 8.4 %copy.47 = f32[32,128,512]{2,1,0:T(8,128)} copy(f32[32,128,512]{2,1,0:T(8,128)} %all-gather.5.cloned.1.call-done) | data formatting | bytes 16777216
  (43 shorter events, 8.2 us)
Async XLA Ops:
  7.2 185.1 %reduce-scatter.7.cloned.1.call-start = ((), (), s32[]{:S(2)}) async-start(), calls=%async_computation.5 | async-start | bytes 10485760 | tf_op jit(solution)/shard_map/reduce_scatter | solution.py:63
  7.2 25.7 %collective-permute-start = (f32[1,1792,128]{2,1,0:T(8,128)}, f32[1,1792,128]{2,1,0:T(8,128)S(1)}, u32[]{:S(2)}, u32[]{:S(2)}) collective-permute-start(f32[1,1792,128]{2,1,0:T(8,128)} %param.7), channel_id=1, source_target_pairs={{0,1},{1,2},{2,3},{3,0},{4,5},{5,6},{6,7},{7,4},{8,9},{9,10},{10,1... | collective-permute-start | bytes 2752520 | tf_op jit(solution)/shard_map/ppermute | solution.py:21
  32.9 23.3 %collective-permute-start.1 = (f32[1,1792,128]{2,1,0:T(8,128)S(1)}, f32[1,1792,128]{2,1,0:T(8,128)S(1)}, u32[]{:S(2)}, u32[]{:S(2)}) collective-permute-start(f32[1,1792,128]{2,1,0:T(8,128)S(1)} %collective-permute-done), channel_id=1, source_target_pairs={{0,1},{1,2},{2,3},{3,0},{4,5},{5,6},{6,7},{7,4},{8,9},{9,10},{10,1... | collective-permute-start | bytes 2752520 | tf_op jit(solution)/shard_map/ppermute | solution.py:21
  56.2 22.6 %collective-permute-start.2 = (f32[1,1792,128]{2,1,0:T(8,128)S(1)}, f32[1,1792,128]{2,1,0:T(8,128)}, u32[]{:S(2)}, u32[]{:S(2)}) collective-permute-start(f32[1,1792,128]{2,1,0:T(8,128)S(1)} %collective-permute-done.1), channel_id=1, source_target_pairs={{0,1},{1,2},{2,3},{3,0},{4,5},{5,6},{6,7},{7,4},{8,9},{9,10},{10,1... | collective-permute-start | bytes 2752520 | tf_op jit(solution)/shard_map/ppermute | solution.py:21
  56.2 22.6 %copy-start.6 = (f32[1,1792,128]{2,1,0:T(8,128)S(1)}, f32[1,1792,128]{2,1,0:T(8,128)}, u32[]{:S(2)}) copy-start(f32[1,1792,128]{2,1,0:T(8,128)} %param.7) | copy-start | bytes 2752516
  90.8 18.3 %copy-start.3 = (f32[7168,128]{1,0:T(8,128)S(1)}, f32[7168,128]{1,0:T(8,128)}, u32[]{:S(2)}) copy-start(f32[7168,128]{1,0:T(8,128)} %fusion.38) | copy-start | bytes 11010052
  109.1 9.2 %copy-start = (f32[1,7168,512]{2,1,0:T(8,128)}, f32[1,7168,512]{2,1,0:T(8,128)S(1)}, u32[]{:S(2)}) copy-start(f32[1,7168,512]{2,1,0:T(8,128)S(1)} %get-tuple-element.18) | copy-start | bytes 44040196
  109.1 9.2 %copy-start.8 = (f32[1,32]{1,0:T(1,128)S(1)}, f32[1,32]{1,0:T(1,128)}, u32[]{:S(2)}) copy-start(f32[1,32]{1,0:T(1,128)} %param.9) | copy-start | bytes 388
  122.9 140.2 %reduce-scatter.5.cloned.1.call-start = ((), (), s32[]{:S(2)}) async-start(), calls=%async_computation.4 | async-start | bytes 4587520 | tf_op jit(solution)/shard_map/reduce_scatter | solution.py:70
  143.0 201.9 %all-gather.3.cloned.1.call-start = ((), (), s32[]{:S(2)}) async-start(), calls=%async_computation.6 | async-start | bytes 10485760 | tf_op jit(solution)/shard_map/all_gather | solution.py:86
  196.9 262.1 %reduce-scatter.11.cloned.1.call-start = ((), (), s32[]{:S(2)}) async-start(), calls=%async_computation.8 | async-start | bytes 10485760 | tf_op jit(solution)/shard_map/reduce_scatter | solution.py:63
  264.7 23.6 %collective-permute-start.3 = (f32[1,1792,128]{1,2,0:T(8,128)S(1)}, f32[1,1792,128]{1,2,0:T(8,128)S(1)}, u32[]{:S(2)}, u32[]{:S(2)}) collective-permute-start(f32[1,1792,128]{1,2,0:T(8,128)S(1)} %fusion.63), channel_id=1, source_target_pairs={{0,1},{1,2},{2,3},{3,0},{4,5},{5,6},{6,7},{7,4},{8,9},{9,10},{10,1... | collective-permute-start | bytes 2752520 | tf_op jit(solution)/shard_map/ppermute | solution.py:21
  288.3 0.9 copy-start.7
  289.2 22.8 %collective-permute-start.4 = (f32[1,1792,128]{1,2,0:T(8,128)S(1)}, f32[1,1792,128]{1,2,0:T(8,128)}, u32[]{:S(2)}, u32[]{:S(2)}) collective-permute-start(f32[1,1792,128]{1,2,0:T(8,128)S(1)} %collective-permute-done.3), channel_id=1, source_target_pairs={{0,1},{1,2},{2,3},{3,0},{4,5},{5,6},{6,7},{7,4},{8,9},{9,10},{10,1... | collective-permute-start | bytes 2752520 | tf_op jit(solution)/shard_map/ppermute | solution.py:21
  312.0 24.1 %collective-permute-start.5 = (f32[1,1792,128]{1,2,0:T(8,128)}, f32[1,1792,128]{1,2,0:T(8,128)}, u32[]{:S(2)}, u32[]{:S(2)}) collective-permute-start(f32[1,1792,128]{1,2,0:T(8,128)} %collective-permute-done.4), channel_id=1, source_target_pairs={{0,1},{1,2},{2,3},{3,0},{4,5},{5,6},{6,7},{7,4},{8,9},{9,10},{10,1... | collective-permute-start | bytes 2752520 | tf_op jit(solution)/shard_map/ppermute | solution.py:21
  344.9 12.4 %copy-start.2 = (f32[7168,128]{0,1:T(8,128)S(1)}, f32[7168,128]{0,1:T(8,128)}, u32[]{:S(2)}) copy-start(f32[7168,128]{0,1:T(8,128)} %fusion.30) | copy-start | bytes 11010052
  375.1 8.4 %copy-start.1 = (f32[1,7168,512]{2,1,0:T(8,128)}, f32[1,7168,512]{2,1,0:T(8,128)S(1)}, u32[]{:S(2)}) copy-start(f32[1,7168,512]{2,1,0:T(8,128)S(1)} %get-tuple-element.16) | copy-start | bytes 44040196
  388.1 142.9 %reduce-scatter.9.cloned.1.call-start = ((), (), s32[]{:S(2)}) async-start(), calls=%async_computation.7 | async-start | bytes 4587520 | tf_op jit(solution)/shard_map/reduce_scatter | solution.py:70
  408.2 50.8 %copy-start.4 = (f32[8,128,512]{2,1,0:T(8,128)S(1)}, f32[8,128,512]{2,1,0:T(8,128)}, u32[]{:S(2)}) copy-start(f32[8,128,512]{2,1,0:T(8,128)} %divide_subtract_fusion) | copy-start | bytes 6291460
  408.2 183.3 %all-gather.5.cloned.1.call-start = ((), (), s32[]{:S(2)}) async-start(), calls=%async_computation.9 | async-start | bytes 10485760 | tf_op jit(solution)/shard_map/all_gather | solution.py:86
  499.0 32.0 %copy-start.5 = (f32[1792,1,128]{0,2,1:T(8,128)S(1)}, f32[1792,1,128]{0,2,1:T(8,128)}, u32[]{:S(2)}) copy-start(f32[1792,1,128]{0,2,1:T(8,128)} %reduce-scatter.5.cloned.1.call-done) | copy-start | bytes 2752516
Sparse Core Ops, SparseCore 0:
  123.0 69.1 reduce-scatter.6
  194.5 68.5 reduce-scatter.4
  264.7 58.5 all-gather.2
  388.2 70.7 reduce-scatter.10
  461.1 69.8 reduce-scatter.8
  533.0 58.4 all-gather.4
